TPU v7x, 32 devices: a whole 2x2x4 slice. The times are simulated.
32 devices in a mesh: groups: 2 (over x), blk: 8 (over z, y), dp: 2 (over core).
Axes of the slice: x: 2, y: 2, z: 4, core: 2. Of those that a mesh axis runs over, the one named last changes fastest.
Arguments:
- particles: bfloat16 [32768, 4096], P(('groups', 'blk', 'dp')), parts along dimension 0, may hold values from -44 to 44
- defocus: int32 [32768], P(('groups', 'blk', 'dp')), parts along dimension 0, may hold values from 0 to 15
- pick_dest: int32 [32768, 1], P(('groups', 'blk', 'dp')), parts along dimension 0, may hold values from 0 to 15; in each aligned block of 1024 rows (0 to 1023, 1024 to 2047, ...) at most 128 rows name the same one
- references: bfloat16 [192, 4096], P(('groups', 'blk')), parts along dimension 0, may hold values from -4 to 4
- ctf_table: float32 [32, 4096], P('groups'), parts along dimension 0, may hold values from 0.1 to 1
Outputs:
- weighted_sums: float32 [192, 4096], P(('groups', 'blk', 'dp')), parts along dimension 0
- ctf_weights: float32 [192, 4096], P(('groups', 'blk', 'dp')), parts along dimension 0
- posterior: float32 [65536, 96], P(('groups', 'blk', 'dp')), parts along dimension 0
There are 2 independent parts, one for each index of `groups`. A program takes and returns all parts, laid end to end along the dimension named above; each array names one. Nothing has to cross between parts.
Inputs may be any that keep to these rules, and one draw needn't show every extreme that they name: `pick_dest`: of the particles that one device holds, at most 128 name any one destination, and in every draw some device sends exactly 128 to one destination.
All inputs are finite; a program needn't handle non-finite values.
Results may differ from a plain program's by a relative error of at most 0.0028.
Values may be sent and summed in bfloat16 or wider, within the bound.
A program may use at most 128 MiB of HBM per device.

v0:
```python
import math

import jax
import jax.numpy as jnp
from jax import lax
from jax.sharding import PartitionSpec as P

PIX = 4096


def lookup(class_ids, table_rows):
    return (class_ids[:, None] == jnp.arange(table_rows, dtype=jnp.int32)[None, :]).astype(
        jnp.float32
    )


def per_device(particles, defocus, pick_dest, references, ctf_table):
    held_rows = particles.shape[0]
    table_rows = ctf_table.shape[0]
    kr_total = references.shape[0] * lax.axis_size("blk")
    device_count = lax.axis_size(("blk", "dp"))
    capacity = max(2, 2 * held_rows // device_count)
    recv_rows = device_count * capacity
    rows_mine = kr_total // device_count
    score_scale = 1.0 / math.sqrt(PIX)
    ctf_square = ctf_table * ctf_table
    own_onehot = lookup(defocus, table_rows)
    modulation = jnp.dot(own_onehot, ctf_table, precision=lax.Precision.HIGHEST)
    modulated = (particles.astype(jnp.float32) * modulation).astype(jnp.bfloat16)
    destination = pick_dest[:, 0]
    dest_hot = (destination[:, None] == jnp.arange(device_count, dtype=jnp.int32)[None, :]).astype(
        jnp.int32
    )
    earlier = jnp.cumsum(dest_hot, axis=0) - dest_hot
    ranking = jnp.sum(earlier * dest_hot, axis=1)
    slot_index = destination * capacity + ranking
    ref_piece = lax.all_gather(references, "blk", axis=0, tiled=True)
    cross_term = lax.dot_general(
        modulated, ref_piece, (((1,), (1,)), ((), ())), preferred_element_type=jnp.float32
    )
    piece_float = ref_piece.astype(jnp.float32)
    quadratic = 0.5 * lax.dot_general(
        ctf_square,
        piece_float * piece_float,
        (((1,), (1,)), ((), ())),
        precision=lax.Precision.HIGHEST,
    )
    scores = score_scale * (
        cross_term - jnp.dot(own_onehot, quadratic, precision=lax.Precision.HIGHEST)
    )
    largest = jnp.max(scores, axis=1, keepdims=True)
    exponent = jnp.exp(scores - largest)
    weights = exponent / jnp.sum(exponent, axis=1, keepdims=True)
    send_weights = jnp.zeros((recv_rows, kr_total), jnp.float32).at[slot_index].set(weights)
    posterior = lax.all_to_all(send_weights, ("blk", "dp"), split_axis=0, concat_axis=0, tiled=True)
    weights_low = weights.astype(jnp.bfloat16)
    weighted_sums = lax.psum_scatter(
        lax.dot_general(
            weights_low, modulated, (((0,), (0,)), ((), ())), preferred_element_type=jnp.float32
        ),
        ("blk", "dp"),
        scatter_dimension=0,
        tiled=True,
    )
    class_sums = lax.dot_general(
        own_onehot, weights, (((0,), (0,)), ((), ())), precision=lax.Precision.HIGHEST
    )
    totals = lax.psum(class_sums, ("blk", "dp"))
    own_sums = lax.dynamic_slice_in_dim(
        totals, lax.axis_index(("blk", "dp")) * rows_mine, rows_mine, 1
    )
    ctf_weights = lax.dot_general(
        own_sums, ctf_square, (((0,), (0,)), ((), ())), precision=lax.Precision.HIGHEST
    )
    return (weighted_sums, ctf_weights, posterior)


def solution(mesh):
    placed = (
        P(("groups", "blk", "dp"), None),
        P(("groups", "blk", "dp")),
        P(("groups", "blk", "dp"), None),
        P(("groups", "blk"), None),
        P("groups", None),
    )
    return jax.shard_map(
        per_device,
        mesh=mesh,
        in_specs=placed,
        out_specs=(
            P(("groups", "blk", "dp"), None),
            P(("groups", "blk", "dp"), None),
            P(("groups", "blk", "dp"), None),
        ),
        check_vma=False,
    )
```

profile of v0, /device:TPU:0, one launch (start us, length us, event | category | flops | bytes accessed | tf_op | source)
XLA Modules:
  0.0 189.7 jit_solution(3554859009608589075)
XLA Ops:
  0.6 34.8 %all-gather = bf16[8,12,4096]{2,1,0:T(8,128)(2,1)S(1)} all-gather(bf16[1,12,4096]{2,1,0:T(8,128)(2,1)} %bitcast.40), channel_id=1, replica_groups=mesh['groups'=2,'blk'=8,'dp'=2] {'blk'}, dimensions={0}, use_global_device_ids=true | all-gather | bytes 884736 | tf_op jit(solution)/shard_map/all_gather | solution.py:37
  35.4 0.2 reshape.38
  35.6 2.3 %fusion.5 = f32[16,96]{1,0:T(8,128)S(1)} fusion(bf16[96,4096]{1,0:T(8,128)(2,1)S(1)} %reshape.38, f32[16,4096]{1,0:T(8,128)} %param.9), kind=kOutput, calls=%fused_computation.7 | convolution fusion | flops 76350976 | bytes 1054720 | tf_op jit(solution)/shard_map/dot_general | solution.py:42
  37.9 9.8 %multiply_convert_fusion = bf16[1024,4096]{1,0:T(8,128)(2,1)S(1)} fusion(bf16[1024,4096]{1,0:T(8,128)(2,1)} %param.5, f32[16,4096]{1,0:T(8,128)} %param.9, s32[1024]{0:T(1024)} %param.6), kind=kOutput, calls=%fused_computation.1 | convolution fusion | flops 817905664 | bytes 17043456 | tf_op jit(solution)/shard_map/dot_general | solution.py:28
  47.7 0.0 copy-start
  47.7 3.2 %copy-done = bf16[1024,4096]{1,0:T(8,128)(2,1)} copy-done((bf16[1024,4096]{1,0:T(8,128)(2,1)}, bf16[1024,4096]{1,0:T(8,128)(2,1)S(1)}, u32[]{:S(2)}) %copy-start) | copy-done | bytes 8388632
  51.0 0.0 copy-start.2
  51.0 0.0 copy-start.3
  51.0 2.7 %fusion.28 = f32[1024,96]{0,1:T(8,128)S(1)} fusion(bf16[1024,4096]{1,0:T(8,128)(2,1)S(1)} %multiply_convert_fusion, bf16[96,4096]{1,0:T(8,128)(2,1)S(1)} %reshape.38), kind=kOutput, calls=%fused_computation.37 | convolution fusion | flops 805306368 | bytes 9568256 | tf_op jit(solution)/shard_map/dot_general | solution.py:38
  53.7 0.0 copy-done.2
  53.7 0.6 fusion.27
  54.3 0.1 fusion.12
  54.3 0.1 fusion.11
  54.4 0.2 copy.20
  54.6 0.0 copy-done.3
  54.6 4.5 %reduce-window.6 = s32[16,8,128]{2,1,0:T(8,128)S(1)} reduce-window(s32[16,8,128]{2,1,0:T(8,128)S(1)} %fusion.24, s32[]{:T(128)} %constant.6.clone.1), window={size=1x1x128 pad=0_0x0_0x127_0}, to_apply=%region_4.5 | reduce-window | flops 2080768 | bytes 131076 | tf_op jit(solution)/shard_map/reduce-window
  59.2 0.1 slice.8
  59.2 0.1 copy.18
  59.4 0.1 copy.19
  59.5 0.1 broadcast_add_fusion
  59.6 3.3 %scatter_custom_fusion = f32[2048,96]{1,0:T(8,128)S(1)} fusion(s32[1024]{0:T(1024)S(1)} %bitcast.45, f32[1024,96]{1,0:T(8,128)S(1)} %copy.20, f32[]{:T(128)} %constant.15.clone.1), kind=kCustom, calls=%fused_computation.9 | custom fusion | bytes 786436 | tf_op jit(solution)/shard_map/scatter | solution.py:54
  63.0 1.2 copy.21
  64.2 5.5 %all-to-all-start = ((f32[16,128,96]{1,2,0:T(8,128)}), f32[16,128,96]{1,2,0:T(8,128)S(1)}, u32[]{:S(2)}, u32[]{:S(2)}) async-start(f32[16,128,96]{1,2,0:T(8,128)} %copy.21), calls=%async_computation | async-start | bytes 1572864 | tf_op jit(solution)/shard_map/all_to_all | solution.py:55
  69.7 0.0 copy-start.1
  69.7 0.0 copy-start.4
  69.7 4.9 %fusion.19 = f32[96,4096]{1,0:T(8,128)S(1)} fusion(bf16[1024,4096]{1,0:T(8,128)(2,1)} %copy-done, f32[1024,96]{0,1:T(8,128)S(1)} %fusion.11), kind=kOutput, calls=%fused_computation.22 | convolution fusion | flops 805404672 | bytes 10354688 | tf_op jit(solution)/shard_map/dot_general | solution.py:58
  74.6 43.0 %fusion = f32[8,4096]{1,0:T(8,128)S(1)} fusion(f32[96,4096]{1,0:T(8,128)S(1)} %fusion.19), kind=kCustom, calls=%all-reduce-scatter | all-reduce-scatter fusion | flops 524289 | bytes 1704448
  117.6 1.3 collective-permute-start
  118.9 1.3 collective-permute-start.1
  120.2 2.2 %collective-permute-start.2 = (f32[8,4096]{1,0:T(8,128)S(1)}, f32[8,4096]{1,0:T(8,128)S(1)}, u32[]{:S(2)}, u32[]{:S(2)}) collective-permute-start(f32[8,4096]{1,0:T(8,128)S(1)} %fusion), channel_id=1, source_target_pairs={{0,3},{1,4},{2,5},{3,6},{4,7},{5,8},{6,9},{7,10},{8,11},{9,12},{10... | collective-permute-start | bytes 393224
  122.4 4.5 %collective-permute-start.3 = (f32[6,4096]{1,0:T(8,128)S(1)}, f32[6,4096]{1,0:T(8,128)S(1)}, u32[]{:S(2)}, u32[]{:S(2)}) collective-permute-start(f32[6,4096]{1,0:T(8,128)S(1)} %slice.10), channel_id=1, source_target_pairs={{0,4},{1,5},{2,6},{3,7},{4,8},{5,9},{6,10},{7,11},{8,12},{9,13},{1... | collective-permute-start | bytes 294920
  126.9 0.5 fusion.10
  127.4 57.7 %psum.7 = f32[16,96]{0,1:T(8,128)S(1)} all-reduce(f32[16,96]{0,1:T(8,128)S(1)} %fusion.10), channel_id=1, replica_groups=mesh['groups'=2,'blk'=8,'dp'=2] {'blk','dp'}, use_global_device_ids=true, to_apply=%region_3.4 | all-reduce | flops 1536 | bytes 12288 | tf_op jit(solution)/shard_map/psum | solution.py:68
  185.1 0.0 copy-done.1
  185.1 0.9 fusion.16
  186.0 0.0 copy-done.4
  186.0 0.6 dynamic-slice.4
  187.3 0.0 collective-permute-done.3
  187.3 0.0 collective-permute-done
  187.3 0.0 collective-permute-done.1
  187.3 0.0 collective-permute-done.2
  187.3 0.8 concatenate
  188.1 0.7 constant_dynamic-slice_fusion
  188.8 0.0 all-to-all-done
  188.8 0.9 copy_bitcast_fusion
  (6 shorter events, 0.1 us)
Async XLA Ops:
  47.7 3.2 %copy-start = (bf16[1024,4096]{1,0:T(8,128)(2,1)}, bf16[1024,4096]{1,0:T(8,128)(2,1)S(1)}, u32[]{:S(2)}) copy-start(bf16[1024,4096]{1,0:T(8,128)(2,1)S(1)} %multiply_convert_fusion) | copy-start | bytes 25165828
  51.0 2.7 %copy-start.2 = (s32[1024]{0:T(1024)S(1)}, s32[1024]{0:T(1024)}, u32[]{:S(2)}) copy-start(s32[1024]{0:T(1024)} %param.6) | copy-start | bytes 12292
  51.0 3.7 %copy-start.3 = (s32[1024,1]{0,1:T(1,128)S(1)}, s32[1024,1]{0,1:T(1,128)}, u32[]{:S(2)}) copy-start(s32[1024,1]{0,1:T(1,128)} %param.7) | copy-start | bytes 12292
  64.2 124.6 %all-to-all-start = ((f32[16,128,96]{1,2,0:T(8,128)}), f32[16,128,96]{1,2,0:T(8,128)S(1)}, u32[]{:S(2)}, u32[]{:S(2)}) async-start(f32[16,128,96]{1,2,0:T(8,128)} %copy.21), calls=%async_computation | async-start | bytes 1572864 | tf_op jit(solution)/shard_map/all_to_all | solution.py:55
  69.7 115.4 %copy-start.1 = (f32[16,4096]{1,0:T(8,128)S(1)}, f32[16,4096]{1,0:T(8,128)}, u32[]{:S(2)}) copy-start(f32[16,4096]{1,0:T(8,128)} %param.9) | copy-start | bytes 786436
  69.7 116.3 %copy-start.4 = (u32[32]{0:T(128)S(1)}, u32[32]{0:T(128)}, u32[]{:S(2)}) copy-start(u32[32]{0:T(128)} %constant.37) | copy-start | bytes 388
  117.6 69.7 %collective-permute-start = (f32[8,4096]{1,0:T(8,128)S(1)}, f32[8,4096]{1,0:T(8,128)S(1)}, u32[]{:S(2)}, u32[]{:S(2)}) collective-permute-start(f32[8,4096]{1,0:T(8,128)S(1)} %fusion), channel_id=1, source_target_pairs={{0,1},{1,2},{2,3},{3,4},{4,5},{5,6},{6,7},{7,8},{8,9},{9,10},{10,1... | collective-permute-start | bytes 393224
  118.9 68.4 %collective-permute-start.1 = (f32[8,4096]{1,0:T(8,128)S(1)}, f32[8,4096]{1,0:T(8,128)S(1)}, u32[]{:S(2)}, u32[]{:S(2)}) collective-permute-start(f32[8,4096]{1,0:T(8,128)S(1)} %fusion), channel_id=1, source_target_pairs={{0,2},{1,3},{2,4},{3,5},{4,6},{5,7},{6,8},{7,9},{8,10},{9,11},{10,... | collective-permute-start | bytes 393224
  120.2 67.1 %collective-permute-start.2 = (f32[8,4096]{1,0:T(8,128)S(1)}, f32[8,4096]{1,0:T(8,128)S(1)}, u32[]{:S(2)}, u32[]{:S(2)}) collective-permute-start(f32[8,4096]{1,0:T(8,128)S(1)} %fusion), channel_id=1, source_target_pairs={{0,3},{1,4},{2,5},{3,6},{4,7},{5,8},{6,9},{7,10},{8,11},{9,12},{10... | collective-permute-start | bytes 393224
  122.4 64.9 %collective-permute-start.3 = (f32[6,4096]{1,0:T(8,128)S(1)}, f32[6,4096]{1,0:T(8,128)S(1)}, u32[]{:S(2)}, u32[]{:S(2)}) collective-permute-start(f32[6,4096]{1,0:T(8,128)S(1)} %slice.10), channel_id=1, source_target_pairs={{0,4},{1,5},{2,6},{3,7},{4,8},{5,9},{6,10},{7,11},{8,12},{9,13},{1... | collective-permute-start | bytes 294920
where the time goes:
time: 190 us
  blocking collectives  136 us (72%)
  matrix products  21.6 us (11%)
  starting transfers between devices  14.8 us (8%)
  local copies, waits for them, and re-layouts  11.5 us (6%)
  other arithmetic  4.82 us (3%)
    psum x1, blocking collectives, per_device(): totals = lax.psum(class_sums, ('blk', 'dp'))  57.7 us
    unnamed x1, blocking collectives  43 us
    all_gather x1, blocking collectives, per_device(): ref_piece = lax.all_gather(references, 'blk', axis=0, tiled=True)  34.8 us
    dot_general x1, matrix products, per_device(): modulation = jnp.dot(own_onehot, ctf_table, precision=lax.Precision.HIGHEST)  9.82 us
    unnamed x4, starting transfers between devices  9.27 us
    all_to_all x1, starting transfers between devices, per_device(): lax.all_to_all(send_weights, ('blk', 'dp'), split_axis=0, concat_axis=0,...  5.49 us
    unnamed x15, local copies, waits for them, and re-layouts  5.48 us
    dot_general x1, matrix products, per_device(): lax.dot_general(weights_low, modulated, (((0,), (0,)), ((), ())), preferr...  4.87 us
  transfers between devices with their start and end apart: 5, of which 0 were waited for; matrix products, arithmetic and copies ran while one was open for 27% of the time, Pallas kernels for 0%

commit v1 on v0

v1 whole, which is shorter than its diff:
```python
import functools
import math

import jax
import jax.numpy as jnp
from jax import lax
from jax.experimental import pallas as pl
from jax.experimental.pallas import tpu as pltpu
from jax.sharding import PartitionSpec as P

F32, BF16 = jnp.float32, jnp.bfloat16
NT = (((1,), (1,)), ((), ()))
HIGH = lax.Precision.HIGHEST
ROW_BLOCK, COL_BLOCK, SUM_BLOCK, PART = 256, 512, 512, 16


def split3(x):
    hi = x.astype(BF16)
    rest = x - hi.astype(F32)
    mid = rest.astype(BF16)
    low = (rest - mid.astype(F32)).astype(BF16)
    return hi, mid, low


def kernel(
    blks, dps, capacity, turned,
    part_ref, defocus_ref, dest_ref, refs_ref, ctf_ref,
    ws_ref, cw_ref, post_ref,
    mod, gath, rfloat, rlow, ctf3, hot, hot_t, score, wlow, wpad, slot,
    post_send, post_recv, pair_send, pair_own, pair_recv, stage, sum_send, sum_recv,
    cls_send, cls_own, cls_pair, cls_sum, cls_recv,
    part_sem, ag_s, ag_r, fw_s, fw_r, post_s, post_r, pair_s, pair_r, sum_s, sum_r,
    cp_s, cp_r, cs_s, cs_r,
):
    devices = blks * dps
    rows, pix = part_ref.shape
    held_refs = refs_ref.shape[0]
    kr = blks * held_refs
    krp = rlow.shape[0]
    mine = kr // devices
    ndef = ctf_ref.shape[0]
    half = pix // 2
    row_blocks, sums = rows // ROW_BLOCK, pix // SUM_BLOCK
    parts = mine * sums // PART
    blk, core = lax.axis_index("blk"), lax.axis_index("dp")
    me = blk * dps + core
    partner = {"dp": 1 - core}

    def particle_copy(r):
        span = pl.ds(pl.multiple_of(r * ROW_BLOCK, ROW_BLOCK), ROW_BLOCK)
        return pltpu.make_async_copy(part_ref.at[span], mod.at[span], part_sem.at[r])

    for r in range(row_blocks):
        particle_copy(r).start()

    barrier = pltpu.get_barrier_semaphore()

    @pl.loop(1, devices)
    def _(k):
        d = lax.rem(me + k, devices)
        pl.semaphore_signal(
            barrier, inc=1, device_id={"blk": d // dps, "dp": lax.rem(d, dps)},
            device_id_type=pl.DeviceIdType.MESH,
        )

    pl.semaphore_wait(barrier, devices - 1)

    def remote(src, dst, send, recv, device):
        return pltpu.make_async_remote_copy(
            src_ref=src, dst_ref=dst, send_sem=send, recv_sem=recv,
            device_id=device, device_id_type=pl.DeviceIdType.MESH,
        )

    my_half = pl.ds(pl.multiple_of(core * half, half), half)
    other_half = pl.ds(pl.multiple_of((1 - core) * half, half), half)

    def gather_copy(k):
        to = lax.rem(blk + k, blks)
        return remote(refs_ref.at[:, my_half], gath.at[blk, :, my_half], ag_s.at[to], ag_r.at[blk], {"blk": to})

    def gather_arrival(b):
        return remote(refs_ref.at[:, my_half], gath.at[b, :, my_half], ag_s.at[b], ag_r.at[b], {"blk": b})

    def forward_copy(b):
        return remote(gath.at[b, :, my_half], gath.at[b, :, my_half], fw_s.at[b], fw_r.at[b], partner)

    def forward_arrival(b):
        return remote(gath.at[b, :, other_half], gath.at[b, :, other_half], fw_s.at[b], fw_r.at[b], partner)

    @pl.loop(1, blks)
    def _(k):
        gather_copy(k).start()

    ctf = ctf_ref[...]
    hi, mid, low = split3(ctf)
    ctf3[...] = jnp.zeros_like(ctf3)
    ctf3[0:ndef, :] = hi
    ctf3[ndef : 2 * ndef, :] = mid
    ctf3[2 * ndef : 3 * ndef, :] = low
    lane_class = lax.broadcasted_iota(jnp.int32, (128, rows), 0)
    hot_f = jnp.where(
        (lax.rem(lane_class, ndef) == defocus_ref[...]) & (lane_class < 3 * ndef), 1.0, 0.0
    ).astype(F32)
    hot_t[...] = hot_f.astype(BF16)
    hot[...] = hot_f.T.astype(BF16)

    def modulate(r):
        span = pl.ds(pl.multiple_of(r * ROW_BLOCK, ROW_BLOCK), ROW_BLOCK)
        particle_copy(r).wait()

        @pl.loop(0, pix // COL_BLOCK)
        def _(c):
            cols = pl.ds(pl.multiple_of(c * COL_BLOCK, COL_BLOCK), COL_BLOCK)
            factor = jnp.dot(hot[span, :], ctf3[:, cols], preferred_element_type=F32)
            mod[span, cols] = (mod[span, cols].astype(F32) * factor).astype(BF16)

    @pl.loop(0, row_blocks)
    def _(r):
        modulate(r)

    before = (
        lax.broadcasted_iota(jnp.int32, (128, 128), 0)
        < lax.broadcasted_iota(jnp.int32, (128, 128), 1)
    )
    before = jnp.where(before, 1.0, 0.0).astype(BF16)
    dest_row = lax.broadcasted_iota(jnp.int32, (devices, 128), 0)
    seen = jnp.zeros((devices, 1), F32)
    for c in range(rows // 128):
        dest = dest_ref[:, c * 128 : (c + 1) * 128]
        dest_hot = jnp.where(dest_row == dest, 1.0, 0.0).astype(F32)
        earlier = jnp.dot(dest_hot.astype(BF16), before, preferred_element_type=F32) + seen
        rank = jnp.sum(earlier * dest_hot, axis=0, keepdims=True)
        slot[:, c * 128 : (c + 1) * 128] = dest * capacity + rank.astype(jnp.int32)
        seen = seen + jnp.sum(dest_hot, axis=1, keepdims=True)

    @pl.loop(1, blks)
    def _(k):
        b = lax.rem(blk + k, blks)
        gather_arrival(b).wait_recv()
        forward_copy(b).start()

    gath[blk] = refs_ref[...]

    @pl.loop(1, blks)
    def _(k):
        forward_arrival(lax.rem(blk + k, blks)).wait_recv()

    if krp > kr:
        rfloat[kr:krp, :] = jnp.zeros((krp - kr, pix), F32)
    for b in range(blks):
        rfloat[b * held_refs : (b + 1) * held_refs, :] = gath[b].astype(F32)

    c_hi, c_mid, c_low = split3(ctf_ref[...] * ctf_ref[...])
    c_parts = jnp.concatenate([c_hi.astype(F32), c_mid.astype(F32), c_low.astype(F32)], axis=0).astype(BF16)
    quad = jnp.zeros((krp, 3 * ndef), F32)
    for c in range(pix // 1024):
        cols = slice(c * 1024, (c + 1) * 1024)
        piece = rfloat[:, cols]
        rlow[:, cols] = piece.astype(BF16)
        square = piece * piece
        s_hi = square.astype(BF16)
        s_low = (square - s_hi.astype(F32)).astype(BF16)
        quad = quad + lax.dot_general(s_hi, c_parts[:, cols], NT, preferred_element_type=F32)
        quad = quad + lax.dot_general(s_low, c_parts[:, cols], NT, preferred_element_type=F32)
    quad = 0.5 * quad

    for r in range(row_blocks):
        span = slice(r * ROW_BLOCK, (r + 1) * ROW_BLOCK)
        cross = lax.dot_general(mod[span, :], rlow[...], NT, preferred_element_type=F32)
        own_quad = jnp.dot(
            quad, hot_t[0 : 3 * ndef, span].astype(F32), precision=HIGH, preferred_element_type=F32
        )
        scores = ((cross.T - own_quad) * (1.0 / math.sqrt(pix)))[0:kr]
        exponent = jnp.exp(scores - jnp.max(scores, axis=0, keepdims=True))
        weights = exponent / jnp.sum(exponent, axis=0, keepdims=True)
        score[:, span] = weights
        wlow[:, span] = weights.astype(BF16)

    def post_copy(d):
        return remote(
            post_send.at[d], post_recv.at[me], post_s.at[d], post_r.at[me],
            {"blk": d // dps, "dp": lax.rem(d, dps)},
        )

    def post_arrival(s):
        return remote(
            post_send.at[s], post_recv.at[s], post_s.at[s], post_r.at[s],
            {"blk": s // dps, "dp": lax.rem(s, dps)},
        )

    def chosen(d):
        places = lax.broadcasted_iota(jnp.int32, (capacity, rows), 0) + d * capacity
        pick = jnp.where(places == slot[...], 1.0, 0.0).astype(BF16)
        pair = (wlow[...], pick) if turned else (pick, wlow[...])
        return lax.dot_general(*pair, NT, preferred_element_type=F32).astype(BF16)

    @pl.loop(1, devices)
    def _(k):
        d = lax.rem(me + k, devices)
        post_send[d] = chosen(d)
        post_copy(d).start()

    pads = devices * 8
    line = lax.broadcasted_iota(jnp.int32, (pads, kr), 0)
    owner_core = jnp.where(line < blks * 8, 1 - core, core)
    owner_blk = lax.rem(line // 8, blks)
    within = lax.rem(line, 8)
    wanted = (owner_blk * dps + owner_core) * mine + within
    select = jnp.where(
        (wanted == lax.broadcasted_iota(jnp.int32, (pads, kr), 1)) & (within < mine), 1.0, 0.0
    ).astype(F32)
    wpad[...] = jnp.dot(select.astype(BF16), wlow[...], preferred_element_type=F32).astype(BF16)

    w_hi, w_mid, w_low = split3(score[...])
    classes = jnp.zeros((kr, 128), F32)
    one_hot = hot_t[0:ndef, :]
    one_hot = jnp.concatenate([one_hot.astype(F32), jnp.zeros((128 - ndef, rows), F32)], axis=0).astype(BF16)
    for w in (w_low, w_mid, w_hi):
        classes = classes + lax.dot_general(w, one_hot, NT, preferred_element_type=F32)
    classes = jnp.dot(select, classes, precision=HIGH, preferred_element_type=F32)
    cls_send[...] = classes[0 : blks * 8].reshape(blks, 8, 128)
    cls_own[...] = classes[blks * 8 :].reshape(blks, 8, 128)

    class_pair = remote(cls_send, cls_pair, cp_s, cp_r, partner)
    class_pair.start()

    def pair_copy(q):
        return remote(pair_send.at[q], pair_recv.at[q], pair_s.at[q], pair_r.at[q], partner)

    @pl.loop(0, sums)
    def _(q):
        cols = pl.ds(pl.multiple_of(q * SUM_BLOCK, SUM_BLOCK), SUM_BLOCK)
        total = jnp.dot(wpad[...], mod[:, cols], preferred_element_type=F32)
        pair_send[q] = total[0 : blks * 8].astype(BF16)
        pair_own[q] = total[blks * 8 :]
        pair_copy(q).start()

    def sum_copy(b, m):
        return remote(
            sum_send.at[b, m], sum_recv.at[blk, m], sum_s.at[b, m], sum_r.at[blk, m], {"blk": b}
        )

    def sum_arrival(b, m):
        return remote(sum_send.at[b, m], sum_recv.at[b, m], sum_s.at[b, m], sum_r.at[b, m], {"blk": b})

    def class_copy(b):
        return remote(cls_sum.at[b], cls_recv.at[blk], cs_s.at[b], cs_r.at[blk], {"blk": b})

    def class_arrival(b):
        return remote(cls_sum.at[b], cls_recv.at[b], cs_s.at[b], cs_r.at[b], {"blk": b})

    class_pair.wait_recv()
    cls_sum[...] = cls_own[...] + cls_pair[...]

    @pl.loop(1, blks)
    def _(k):
        class_copy(lax.rem(blk + k, blks)).start()

    sent = 0
    for q in range(sums):
        pair_copy(q).wait_recv()
        chip = pair_own[q] + pair_recv[q].astype(F32)
        stage[:, q * mine : (q + 1) * mine, :] = chip.reshape(blks, 8, SUM_BLOCK)[:, 0:mine, :]
        while (sent + 1) * PART <= (q + 1) * mine:
            sum_send[:, sent] = stage[:, sent * PART : (sent + 1) * PART, :].astype(BF16)

            @pl.loop(1, blks)
            def _(k, sent=sent):
                sum_copy(lax.rem(blk + k, blks), sent).start()

            sent += 1

    kept = chosen(me).astype(F32)
    post_ref[pl.ds(pl.multiple_of(me * capacity, capacity), capacity), :] = kept.T if turned else kept

    @pl.loop(1, devices)
    def _(k):
        s = lax.rem(me + k, devices)
        post_arrival(s).wait_recv()
        got = post_recv[s].astype(F32)
        post_ref[pl.ds(pl.multiple_of(s * capacity, capacity), capacity), :] = got.T if turned else got

    cls_recv[blk] = cls_sum[blk]

    @pl.loop(1, blks)
    def _(k):
        class_arrival(lax.rem(blk + k, blks)).wait_recv()

    totals = jnp.sum(cls_recv[...], axis=0)[:, 0:ndef]
    ctf_now = ctf_ref[...]
    cw_ref[...] = jnp.dot(totals, ctf_now * ctf_now, precision=HIGH, preferred_element_type=F32)[0:mine]

    for m in range(parts):
        lines = slice(m * PART, (m + 1) * PART)

        def add(k, acc, m=m):
            b = lax.rem(blk + k, blks)
            sum_arrival(b, m).wait_recv()
            return acc + sum_recv[b, m].astype(F32)

        stage[0, lines, :] = lax.fori_loop(1, blks, add, stage[blk, lines, :])
    for q in range(sums):
        ws_ref[:, q * SUM_BLOCK : (q + 1) * SUM_BLOCK] = stage[0, q * mine : (q + 1) * mine, :]

    class_pair.wait_send()

    @pl.loop(1, devices)
    def _(k):
        post_copy(lax.rem(me + k, devices)).wait_send()

    @pl.loop(0, sums)
    def _(q):
        pair_copy(q).wait_send()

    @pl.loop(1, blks)
    def _(k):
        b = lax.rem(blk + k, blks)
        gather_copy(k).wait_send()
        forward_copy(b).wait_send()
        class_copy(b).wait_send()
        for m in range(parts):
            sum_copy(b, m).wait_send()


def per_device(particles, defocus, pick_dest, references, ctf_table):
    rows, pix = particles.shape
    blks, dps = lax.axis_size("blk"), lax.axis_size("dp")
    devices = blks * dps
    held = references.shape[0]
    kr = held * blks
    krp = -(-kr // 128) * 128
    capacity = max(2, 2 * rows // devices)
    mine = kr // devices
    turned = kr % 128 != 0 and capacity % 128 == 0
    sums = pix // SUM_BLOCK
    parts = mine * sums // PART
    block = (kr, capacity) if turned else (capacity, kr)
    vmem = pl.BlockSpec(memory_space=pltpu.VMEM)
    dma = pltpu.SemaphoreType.DMA
    V = pltpu.VMEM
    return tuple(
        pl.pallas_call(
            functools.partial(kernel, blks, dps, capacity, turned),
            out_shape=(
                jax.ShapeDtypeStruct((mine, pix), F32),
                jax.ShapeDtypeStruct((mine, pix), F32),
                jax.ShapeDtypeStruct((devices * capacity, kr), F32),
            ),
            in_specs=[pl.BlockSpec(memory_space=pl.ANY), vmem, vmem, vmem, vmem],
            out_specs=(vmem, vmem, vmem),
            scratch_shapes=[
                V((rows, pix), BF16), V((blks, held, pix), BF16), V((krp, pix), F32), V((krp, pix), BF16),
                V((128, pix), BF16), V((rows, 128), BF16), V((128, rows), BF16),
                V((kr, rows), F32), V((kr, rows), BF16), V((devices * 8, rows), BF16), V((1, rows), jnp.int32),
                V((devices, *block), BF16), V((devices, *block), BF16),
                V((sums, blks * 8, SUM_BLOCK), BF16), V((sums, blks * 8, SUM_BLOCK), F32),
                V((sums, blks * 8, SUM_BLOCK), BF16),
                V((blks, mine * sums, SUM_BLOCK), F32),
                V((blks, parts, PART, SUM_BLOCK), BF16), V((blks, parts, PART, SUM_BLOCK), BF16),
                V((blks, 8, 128), F32), V((blks, 8, 128), F32), V((blks, 8, 128), F32),
                V((blks, 8, 128), F32), V((blks, 8, 128), F32),
                dma((rows // ROW_BLOCK,)), dma((blks,)), dma((blks,)), dma((blks,)), dma((blks,)),
                dma((devices,)), dma((devices,)), dma((sums,)), dma((sums,)),
                dma((blks, parts)), dma((blks, parts)), dma, dma, dma((blks,)), dma((blks,)),
            ],
            compiler_params=pltpu.CompilerParams(
                collective_id=0, has_side_effects=True, vmem_limit_bytes=60 * 1024 * 1024
            ),
        )(particles, defocus.reshape(1, rows), pick_dest.reshape(1, rows), references, ctf_table)
    )


def solution(mesh):
    placed = (
        P(("groups", "blk", "dp"), None),
        P(("groups", "blk", "dp")),
        P(("groups", "blk", "dp"), None),
        P(("groups", "blk"), None),
        P("groups", None),
    )
    return jax.shard_map(
        per_device,
        mesh=mesh,
        in_specs=placed,
        out_specs=(
            P(("groups", "blk", "dp"), None),
            P(("groups", "blk", "dp"), None),
            P(("groups", "blk", "dp"), None),
        ),
        check_vma=False,
    )
```

time: 190 us -> 51.5 us (0.27)
  blocking collectives: 136 us -> 0 us
  Pallas kernels: 0 us -> 44.9 us
  matrix products: 21.6 us -> 0 us
  starting transfers between devices: 14.8 us -> 0 us
  local copies, waits for them, and re-layouts: 11.5 us -> 5.57 us
  other arithmetic: 4.82 us -> 0 us
    psum x1 -> x0, blocking collectives: 57.7 us -> none  [per_device(): totals = lax.psum(class_sums, ('blk', 'dp'))]
    pallas_call x0 -> x1, Pallas kernels: none -> 44.9 us  [per_device(): pl.pallas_call(functools.partial(kernel, blks, dps, capacity, turned), ou...]
    unnamed x1 -> x0, blocking collectives: 43 us -> none
    all_gather x1 -> x0, blocking collectives: 34.8 us -> none  [per_device(): ref_piece = lax.all_gather(references, 'blk', axis=0, tiled=True)]
    dot_general x7 -> x0, matrix products: 21.6 us -> none  [the longest x1 9.82 us: per_device(): modulation = jnp.dot(own_onehot, ctf_table, precision=lax.Precision.HIGHEST)]
    unnamed x4 -> x0, starting transfers between devices: 9.27 us -> none
    all_to_all x1 -> x0, starting transfers between devices: 5.49 us -> none  [per_device(): lax.all_to_all(send_weights, ('blk', 'dp'), split_axis=0, concat_axis=0,...]
    another operation x3 -> x0, other arithmetic: 4.64 us -> none
  transfers between devices with their start and end apart: 5 -> 0, of which waited for: 0 -> 0; matrix products, arithmetic and copies ran while one was open for 27% -> 0% of each run, Pallas kernels for 0% -> 0%
where the time goes in v1:
time: 51.5 us; the launch traced here: 51.1 us
  Pallas kernels  44.9 us (87%)
  local copies, waits for them, and re-layouts  5.57 us (11%)
  between operations  0.64 us (1%)
    pallas_call x1, Pallas kernels, per_device(): pl.pallas_call(functools.partial(kernel, blks, dps, capacity, turned), ou...  44.9 us
    unnamed x2, local copies, waits for them, and re-layouts  3.13 us
    pallas_call x1, local copies, waits for them, and re-layouts, per_device(): pl.pallas_call(functools.partial(kernel, blks, dps, capacity, turned), ou...  2.43 us

profile of v1, /device:TPU:0, one launch (start us, length us, event | category | flops | bytes accessed | tf_op | source)
XLA Modules:
  0.0 51.1 jit_solution(3326367487804464868)
XLA Ops:
  0.6 44.9 %shard_map.76 = (f32[6,4096]{1,0:T(8,128)}, f32[6,4096]{1,0:T(8,128)}, f32[2048,96]{1,0:T(8,128)}) custom-call(bf16[1024,4096]{1,0:T(8,128)(2,1)} %part_ref.1, s32[1,1024]{1,0:T(1,128)} %bitcast.2, s32[1,1024]{1,0:T(1,128)} %bitcast.3, bf16[12,4096]{1,0:T(8,128)(2,1)} %refs_ref.1, f32[16,4096]{1,0:T(8,128)} %ctf_ref.1), custom_call_target="tpu_custom_call" | custom-call | tf_op jit(solution)/shard_map/pallas_call | solution.py:342
  45.5 2.4 %copy.8 = f32[2048,96]{0,1:T(8,128)} copy(f32[2048,96]{1,0:T(8,128)} %get-tuple-element.5) | data formatting | bytes 1572864 | tf_op jit(solution)/shard_map/pallas_call | solution.py:342
  48.0 1.6 %copy.11 = f32[6,4096]{1,0:T(8,128)} copy(f32[6,4096]{1,0:T(8,128)} %get-tuple-element.9) | data formatting | bytes 196608
  49.5 1.6 %copy.12 = f32[6,4096]{1,0:T(8,128)} copy(f32[6,4096]{1,0:T(8,128)} %get-tuple-element.10) | data formatting | bytes 196608
